TPU v7x, 512 devices: a whole 4x4x16 slice. The times are simulated.
512 devices in a mesh: rows: 128 (over x, y, z_hi, core), ch: 4 (over z_lo).
Axes of the slice: x: 4, y: 4, z: 16 (z_hi: 4, z_lo: 4; z = z_hi * 4 + z_lo), core: 2. Of those that a mesh axis runs over, the one named last changes fastest.
Arguments:
- pixels: bfloat16 [256, 1024, 256], P('ch', 'rows'), may hold values from -24 to 24
- conv_gain: float32 [256], replicated, may hold values from 0.25 to 1.75
- expand_weight: bfloat16 [256, 1024], replicated, may hold values from -0.375 to 0.375
- depth_kernel: bfloat16 [3, 3, 1024], replicated, may hold values from -2 to 2
- shrink_weight: bfloat16 [1024, 256], replicated, may hold values from -0.1875 to 0.1875
- block_gain: float32 [256], replicated, may hold values from 0.25 to 1.75
- block_qkv: bfloat16 [256, 768], replicated, may hold values from -0.375 to 0.375
- block_merge: bfloat16 [256, 256], replicated, may hold values from -0.375 to 0.375
- block_bias: float32 [8, 15, 15], replicated, may hold values from -3 to 400
- grid_gain: float32 [256], replicated, may hold values from 0.25 to 1.75
- grid_qkv: bfloat16 [256, 768], replicated, may hold values from -0.375 to 0.375
- grid_merge: bfloat16 [256, 256], replicated, may hold values from -0.375 to 0.375
- grid_bias: float32 [8, 15, 15], replicated, may hold values from -3 to 400
- mlp_gain: float32 [256], replicated, may hold values from 0.25 to 1.75
- mlp_up: bfloat16 [256, 1024], replicated, may hold values from -0.375 to 0.375
- mlp_down: bfloat16 [1024, 256], replicated, may hold values from -0.1875 to 0.1875
Outputs:
- block_output: bfloat16 [256, 1024, 256], P('ch', 'rows')
All inputs are finite; a program needn't handle non-finite values.
Results may differ from a plain program's by a relative error of at most 0.02.
Values may be sent and summed in bfloat16 or wider, within the bound.
A program may use at most 64 MiB of HBM per device.

v0:
```python
import functools
import math

import jax
import jax.numpy as jnp
import numpy as np
from jax import lax
from jax.experimental import pallas as pl
from jax.experimental.pallas import tpu as pltpu
from jax.sharding import PartitionSpec as P

WIN = 8
HALF = 64
EPS = 1e-05
F32 = jnp.float32
BF16 = jnp.bfloat16
MESH = pl.DeviceIdType.MESH
VM = pl.BlockSpec(memory_space=pltpu.VMEM)
LIMIT = 56 * 1024 * 1024


def dot(a, b, dims=((1,), (0,))):
    return lax.dot_general(a, b, (dims, ((), ())), preferred_element_type=F32)


def norm(values, gain):
    middle = jnp.mean(values, axis=-1, keepdims=True)
    off = values - middle
    spread = jnp.mean(off * off, axis=-1, keepdims=True)
    return (off * lax.rsqrt(spread + EPS) * gain).astype(BF16)


def gelu(v):
    return 0.5 * v * (1.0 + lax.erf(v * np.float32(math.sqrt(0.5))))


def rounded(v):
    return v.astype(BF16).astype(F32)


def swapped(v):
    return pltpu.roll(v, HALF, 1)


def pick_rows(lanes):
    width = 4 * lanes * WIN
    first = np.zeros((lanes * 40, width), np.float32)
    second = np.zeros((lanes * 40, width), np.float32)
    mask = np.zeros((lanes * 40, 128), np.float32)
    for j in range(lanes):
        for q in range(40):
            if q < 32:
                col = (q // 8 * lanes + j) * 8 + q % 8
            else:
                col = ((q - 32) % 4 * lanes + j) * 8 + (-1 if q < 36 else 8)
            row = j * 40 + q
            if col < 0:
                second[row, width - 1] = 1
                mask[row, HALF:] = 1
            elif col >= width:
                second[row, 0] = 1
                mask[row, :HALF] = 1
            else:
                first[row, col] = 1
    return first, second, mask


def prep_body(px, first, second, mask, send):
    half = px.shape[2] // 2
    lanes = send.shape[0]
    for y in range(WIN):
        low, high = px[y, :, :half], px[y, :, half:]
        main = dot(first[...], jnp.concatenate([low, high], 0), ((1,), (1,)))
        rim = dot(second[...], jnp.concatenate([high, low], 0), ((1,), (1,)))
        rows = (main + rim * mask[...]).astype(BF16)
        for j in range(lanes):
            send[j, y] = rows[j * 40 : (j + 1) * 40]


def bias_fill(table, bias):
    t = table[...]
    shifted = [t if z == 0 else pltpu.roll(t, 256 - z * 16, 1) for z in range(WIN)]
    rows = jnp.concatenate([s[:, :128] for s in shifted], 0)
    r = lax.broadcasted_iota(jnp.int32, (128, 128), 0)
    c = lax.broadcasted_iota(jnp.int32, (128, 128), 1)
    m, j = r >> 4, r & 15
    y, x = (c >> 3) & 7, c & 7
    for v in range(WIN):
        onehot = jnp.where((m == 7 - y) & (j == v - x + 7), 1.0, 0.0).astype(F32)
        got = lax.dot_general(
            rows, onehot, (((1,), (0,)), ((), ())),
            precision=lax.Precision.HIGHEST, preferred_element_type=F32,
        )
        bias[:, v] = got.reshape(WIN, WIN, 128)


def attend_pair(x, gain, qkv, merge, bias):
    channels = x.shape[1]
    depth = channels // WIN
    proj = dot(norm(x, gain), qkv)
    q = proj[:, :channels].astype(BF16)
    head = lax.broadcasted_iota(jnp.int32, (WIN, channels), 0)
    place = lax.broadcasted_iota(jnp.int32, (WIN, channels), 1)
    own = jnp.where((place >= head * depth) & (place < head * depth + depth), 1.0, 0.0)

    def spread(rows):
        wide = rounded(rows)[:, None, :] * own[None]
        return wide.reshape(64 * WIN, channels).astype(BF16)

    keys = [spread(proj[w * 64 : w * 64 + 64, channels : 2 * channels]) for w in (0, 1)]
    vals = [spread(proj[w * 64 : w * 64 + 64, 2 * channels :]) for w in (0, 1)]
    raw = [dot(k, q, ((1,), (1,))) for k in keys]
    lane = lax.broadcasted_iota(jnp.int32, raw[0].shape, 1)
    scores = jnp.where(lane < 64, raw[0], raw[1]) * np.float32(1.0 / math.sqrt(depth))
    scores = scores.reshape(64, WIN, 128) + bias[...].reshape(64, WIN, 128)
    raised = jnp.exp(scores - jnp.max(scores, axis=0, keepdims=True))
    weights = raised * (1.0 / jnp.sum(raised, axis=0, keepdims=True))
    weights = jnp.transpose(weights.reshape(512, 128)).astype(BF16)
    heads = jnp.concatenate([dot(weights[w * 64 : w * 64 + 64], vals[w]) for w in (0, 1)], 0)
    return rounded(x + dot(heads.astype(BF16), merge))


def block_body(
    edge, got, conv_gain, expand, taps, shrink, gain, qkv, merge, table, send,
    tokens, normed, acc, bias, done,
):
    lanes = got.shape[0]
    lane = lax.broadcasted_iota(jnp.int32, (400, 128), 1)
    row = lax.broadcasted_iota(jnp.int32, (400, 128), 0)
    keep = ((row >= 40) | (edge[0] == 0)) & ((row < 360) | (edge[1] == 0))
    for i in range(0, lanes, 2):
        a = jnp.where(keep, got[i].astype(F32).reshape(400, 128), 0.0)
        b = jnp.where(keep, got[i + 1].astype(F32).reshape(400, 128), 0.0)
        cols = slice(i * HALF, i * HALF + 128)
        tokens[:400, cols] = jnp.where(lane < HALF, a, swapped(b))
        tokens[400:, cols] = jnp.where(lane < HALF, swapped(a), b)
    for half in (0, 1):
        normed[half * 400 : half * 400 + 400] = norm(
            tokens[half * 400 : half * 400 + 400], conv_gain[...]
        )
    for half in (0, 1):
        for y in range(WIN):
            base = half * 400 + (y + 1) * 40
            acc[half * 256 + y * 32 : half * 256 + y * 32 + 32] = tokens[base : base + 32]

    width = 128
    inner = lax.broadcasted_iota(jnp.int32, (WIN, WIN, width), 1)

    def chunk(n, _):
        at = pl.ds(pl.multiple_of(n * width, width), width)
        kernel = taps[:, at]
        for half in (0, 1):
            wide = rounded(gelu(dot(normed[half * 400 : half * 400 + 400], expand[:, at])))
            wide = wide.reshape(10, 5, 8, width)

            def column(v, tile):
                total = None
                for u in range(3):
                    term = wide[u : u + WIN, tile] * kernel[u * 3 + v][None, None, :]
                    total = term if total is None else total + term
                return total

            left_rim, right_rim = column(0, 4), column(2, 4)
            parts = []
            for b in range(4):
                left = jnp.where(
                    inner == 0, left_rim[:, b : b + 1], pltpu.roll(column(0, b), 1, 1)
                )
                right = jnp.where(
                    inner == 7, right_rim[:, 4 + b : 5 + b], pltpu.roll(column(2, b), 7, 1)
                )
                parts.append(column(1, b) + left + right)
            summed = jnp.stack(parts, axis=1).reshape(256, width)
            narrow = dot(gelu(summed).astype(BF16), shrink[at, :])
            acc[half * 256 : half * 256 + 256] += narrow
        return _

    lax.fori_loop(0, expand.shape[1] // width, chunk, 0)
    bias_fill(table, bias)
    channels = acc.shape[1]

    def pair(n, _):
        groups = []
        for w in (0, 1):
            b = n * 2 + w
            base = (b >> 2) * 256 + (b & 3) * 8
            groups += [acc[pl.ds(pl.multiple_of(base + y * 32, 8), 8)] for y in range(WIN)]
        x = rounded(jnp.concatenate(groups, 0))
        out = attend_pair(x, gain[...], qkv[...], merge[...], bias)
        for w in (0, 1):
            b = n * 2 + w
            for y in range(WIN):
                here = slice(w * 64 + y * 8, w * 64 + y * 8 + 8)
                at = pl.ds(pl.multiple_of(y * 64 + b * 8, 8), 8)
                for c in range(channels // 128):
                    done[c, at] = out[here, c * 128 : c * 128 + 128]
        return _

    lax.fori_loop(0, 4, pair, 0)
    for x in range(WIN):
        for c in range(channels // 128):
            part = done[c, pl.ds(x, 64, stride=8)]
            send[x, :, c * 128 : c * 128 + 128] = part.astype(BF16)


def grid_body(got, gain, qkv, merge, table, mlp_gain, up, down, send, tokens, bias):
    for a in range(WIN):
        tokens[a] = got[a].astype(F32)
    bias_fill(table, bias)
    channels = tokens.shape[2]
    lane = lax.broadcasted_iota(jnp.int32, (64, 128), 1)

    def pair(n, _):
        halves = [
            tokens[:, pl.ds(pl.multiple_of(n * 8 + w * 32, 8), 8)].reshape(64, channels)
            for w in (0, 1)
        ]
        x = attend_pair(
            jnp.concatenate(halves, 0), gain[...], qkv[...], merge[...], bias
        )
        hidden = gelu(dot(norm(x, mlp_gain[...]), up[...])).astype(BF16)
        out = rounded(x + dot(hidden, down[...]))
        for c in range(0, channels, 128):
            low, high = out[:64, c : c + 128], out[64:, c : c + 128]
            even = jnp.where(lane < HALF, low, swapped(high))
            odd = jnp.where(lane < HALF, swapped(low), high)
            j = c // HALF
            send[:, j, n] = even.reshape(WIN, WIN, 128).astype(BF16)
            send[:, j + 1, n] = odd.reshape(WIN, WIN, 128).astype(BF16)
        return _

    lax.fori_loop(0, 4, pair, 0)


def finish_body(got, out, rows):
    lanes = got.shape[1]
    columns = WIN * WIN * lanes
    for x in range(WIN):
        for j in range(lanes):
            rows[pl.ds(j * 8 + x, 32, stride=8 * lanes)] = got[x, j].astype(F32).reshape(32, 128)
    for y in range(4):
        flat = jnp.transpose(rows[y * columns : (y + 1) * columns]).astype(BF16)
        out[y] = flat[:HALF]
        out[y + 4] = flat[HALF:]


def greet(partners):
    barrier = pltpu.get_barrier_semaphore()
    for partner in partners:
        pl.semaphore_signal(barrier, inc=1, device_id=partner, device_id_type=MESH)
    pl.semaphore_wait(barrier, len(partners))


def spread_body(bands, lanes, send, got, send_sem, recv_sem, own_sem):
    band, lane = lax.axis_index("rows"), lax.axis_index("ch")
    below, above = lax.rem(band + 1, bands), lax.rem(band + bands - 1, bands)
    others = [lax.rem(lane + d, lanes) for d in range(1, lanes)]
    everyone = [lax.rem(lane + d, lanes) for d in range(lanes)]
    greet(
        [(band, j) for j in others]
        + [(below, j) for j in everyone]
        + [(above, j) for j in everyone]
    )

    def remote(j, d, kind, row, source, mine):
        if kind == 0:
            src, dst = send.at[j], got.at[mine, pl.ds(1, WIN)]
        else:
            src = send.at[j, WIN - 1 if kind == 1 else 0]
            dst = got.at[mine, 0 if kind == 1 else WIN + 1]
        return pltpu.make_async_remote_copy(
            src_ref=src, dst_ref=dst, send_sem=send_sem.at[kind, d],
            recv_sem=recv_sem.at[kind, mine], device_id=(row, j), device_id_type=MESH,
        )

    copies = []
    for d in range(1, lanes):
        copies.append(remote(lax.rem(lane + d, lanes), d, 0, band, None, lane))
    for kind, row in ((1, below), (2, above)):
        for d in range(lanes):
            copies.append(remote(lax.rem(lane + d, lanes), d, kind, row, None, lane))
    for copy in copies:
        copy.start()
    own = pltpu.make_async_copy(send.at[lane], got.at[lane, pl.ds(1, WIN)], own_sem)
    own.start()
    own.wait()
    for d in range(1, lanes):
        j = lax.rem(lane + d, lanes)
        remote(j, d, 0, band, None, j).wait_recv()
    for kind, row in ((1, below), (2, above)):
        for d in range(lanes):
            j = lax.rem(lane + d, lanes)
            remote(j, d, kind, row, None, j).wait_recv()
    for copy in copies:
        copy.wait_send()


def regroup_body(step, send, got, send_sem, recv_sem, own_sem):
    band, lane = lax.axis_index("rows"), lax.axis_index("ch")
    slot, rest = band // step, lax.rem(band, step)
    slots = [lax.rem(slot + d, WIN) for d in range(WIN)]
    greet([(s * step + rest, lane) for s in slots[1:]])

    def remote(d, mine):
        return pltpu.make_async_remote_copy(
            src_ref=send.at[slots[d]], dst_ref=got.at[mine], send_sem=send_sem.at[d],
            recv_sem=recv_sem.at[mine], device_id=(slots[d] * step + rest, lane),
            device_id_type=MESH,
        )

    copies = [remote(d, slot) for d in range(1, WIN)]
    for copy in copies:
        copy.start()
    own = pltpu.make_async_copy(send.at[slot], got.at[slot], own_sem)
    own.start()
    own.wait()
    for d in range(1, WIN):
        remote(d, slots[d]).wait_recv()
    for copy in copies:
        copy.wait_send()


def home_body(step, lanes, send, got, send_sem, recv_sem, own_sem):
    band, lane = lax.axis_index("rows"), lax.axis_index("ch")
    slot, rest = band // step, lax.rem(band, step)
    peers = [
        (d, e, lax.rem(slot + d, WIN), lax.rem(lane + e, lanes))
        for d in range(WIN)
        for e in range(lanes)
        if d or e
    ]
    greet([(s * step + rest, j) for _, _, s, j in peers])

    def remote(d, e, s, j, slot_at, lane_at):
        return pltpu.make_async_remote_copy(
            src_ref=send.at[s, j], dst_ref=got.at[slot_at, lane_at],
            send_sem=send_sem.at[d, e], recv_sem=recv_sem.at[slot_at, lane_at],
            device_id=(s * step + rest, j), device_id_type=MESH,
        )

    copies = [remote(d, e, s, j, slot, lane) for d, e, s, j in peers]
    for copy in copies:
        copy.start()
    own = pltpu.make_async_copy(send.at[slot, lane], got.at[slot, lane], own_sem)
    own.start()
    own.wait()
    for d, e, s, j in peers:
        remote(d, e, s, j, s, j).wait_recv()
    for copy in copies:
        copy.wait_send()


def local(body, name, shape, dtype, operands, scratch, smem=0):
    return pl.pallas_call(
        body,
        out_shape=jax.ShapeDtypeStruct(shape, dtype),
        in_specs=[pl.BlockSpec(memory_space=pltpu.SMEM)] * smem + [VM] * (len(operands) - smem),
        out_specs=VM,
        scratch_shapes=scratch,
        compiler_params=pltpu.CompilerParams(vmem_limit_bytes=LIMIT),
        name=name,
    )(*operands)


def exchange(body, name, number, shape, operand, sems):
    return pl.pallas_call(
        body,
        out_shape=jax.ShapeDtypeStruct(shape, BF16),
        in_specs=[VM],
        out_specs=VM,
        scratch_shapes=[
            pltpu.SemaphoreType.DMA(sems),
            pltpu.SemaphoreType.DMA(sems),
            pltpu.SemaphoreType.DMA,
        ],
        compiler_params=pltpu.CompilerParams(
            collective_id=number, has_side_effects=True, vmem_limit_bytes=LIMIT
        ),
        name=name,
    )(operand)


def flat_table(bias):
    return jnp.pad(bias, ((0, 0), (0, 1), (0, 1))).reshape(bias.shape[0], 256)


def shards(
    pixels, conv_gain, expand_weight, depth_kernel, shrink_weight,
    block_gain, block_qkv, block_merge, block_bias,
    grid_gain, grid_qkv, grid_merge, grid_bias, mlp_gain, mlp_up, mlp_down,
):
    lanes, bands = lax.axis_size("ch"), lax.axis_size("rows")
    channels = expand_weight.shape[0]
    hidden = expand_weight.shape[1]
    columns = pixels.shape[2]
    step = bands // WIN
    band = lax.axis_index("rows")
    edge = jnp.stack([band == 0, band == bands - 1]).astype(jnp.int32)
    first, second, mask = pick_rows(lanes)
    px = jnp.transpose(pixels, (1, 0, 2))
    sent = local(
        prep_body, "prep", (lanes, WIN, 40, 128), BF16,
        [px, jnp.asarray(first, BF16), jnp.asarray(second, BF16), jnp.asarray(mask, F32)], [],
    )
    got = exchange(
        functools.partial(spread_body, bands, lanes), "spread", 1,
        (lanes, WIN + 2, 40, 128), sent, (3, lanes),
    )
    taps = depth_kernel.astype(F32).reshape(9, hidden)
    sent = local(
        block_body, "block", (WIN, 64, channels), BF16,
        [
            edge, got, conv_gain[None], expand_weight, taps, shrink_weight,
            block_gain[None], block_qkv, block_merge, flat_table(block_bias),
        ],
        [
            pltpu.VMEM((800, channels), F32),
            pltpu.VMEM((800, channels), BF16),
            pltpu.VMEM((512, channels), F32),
            pltpu.VMEM((WIN, WIN, WIN, 128), F32),
            pltpu.VMEM((channels // 128, 512, 128), F32),
        ],
        smem=1,
    )
    got = exchange(
        functools.partial(regroup_body, step), "regroup", 2, sent.shape, sent, (WIN,)
    )
    sent = local(
        grid_body, "grid", (WIN, lanes, 4, WIN, 128), BF16,
        [
            got, grid_gain[None], grid_qkv, grid_merge, flat_table(grid_bias),
            mlp_gain[None], mlp_up, mlp_down,
        ],
        [
            pltpu.VMEM((WIN, 64, channels), F32),
            pltpu.VMEM((WIN, WIN, WIN, 128), F32),
        ],
    )
    got = exchange(
        functools.partial(home_body, step, lanes), "home", 3, sent.shape, sent, (WIN, lanes)
    )
    out = local(
        finish_body, "finish", (WIN, HALF, columns), BF16, [got],
        [pltpu.VMEM((4 * columns, 128), F32)],
    )
    return jnp.transpose(out, (1, 0, 2))


def solution(mesh):
    in_specs = (P("ch", "rows", None),) + (P(),) * 15
    return jax.shard_map(
        shards, mesh=mesh, in_specs=in_specs, out_specs=P("ch", "rows", None), check_vma=False
    )
```

profile of v0, /device:TPU:1, one launch (start us, length us, event | category | flops | bytes accessed | tf_op | source)
XLA Modules:
  0.0 89.3 jit_solution(16597721840142959039)
XLA Ops:
  0.0 0.6 add_convert_fusion.edge
  0.6 1.7 %copy.27 = bf16[64,8,256]{2,0,1:T(8,128)(2,1)} copy(bf16[64,8,256]{2,1,0:T(8,128)(2,1)} %param.19) | data formatting | bytes 524288 | tf_op args[0]
  2.3 2.2 %prep.1.send = bf16[4,8,40,128]{3,2,1,0:T(8,128)(2,1)} custom-call(bf16[8,64,256]{2,1,0:T(8,128)(2,1)} %bitcast.10, bf16[160,128]{1,0:T(8,128)(2,1)} %constant.18.clone.first, bf16[160,128]{1,0:T(8,128)(2,1)} %constant.19.clone.second, f32[160,128]{1,0:T(8,128)} %constant.20.clone.mask), custom_call_target="tpu_custom_call" | custom-call | tf_op jit(solution)/shard_map/prep/pallas_call | solution.py:354
  4.6 0.0 copy-start
  4.6 26.5 %spread.1.got = bf16[4,10,40,128]{3,2,1,0:T(8,128)(2,1)} custom-call(bf16[4,8,40,128]{3,2,1,0:T(8,128)(2,1)} %prep.1.send), custom_call_target="tpu_custom_call" | custom-call | tf_op jit(solution)/shard_map/spread/pallas_call | solution.py:366
  31.1 0.0 copy-done
  31.1 0.0 copy-start.2
  31.1 0.7 reshape.13.table
  31.8 0.0 copy-done.2
  31.9 0.6 reshape.16.taps
  32.5 14.3 %block.1.send = bf16[8,64,256]{2,1,0:T(8,128)(2,1)} custom-call(s32[2]{0:T(128)} %add_convert_fusion.edge, bf16[4,10,40,128]{3,2,1,0:T(8,128)(2,1)} %spread.1.got, f32[1,256]{1,0:T(1,128)} %bitcast.14, bf16[256,1024]{1,0:T(8,128)(2,1)} %expand.1, f32[9,1024]{1,0:T(8,128)} %reshape.16.taps, bf16[1024,256]{1,0:T(8,128)(2,1)} %shrink.1, f32[1,256]{1,0:T(1,128)} %bitcast.15, ...), custom_call_target="tpu_custom_call" | custom-call | tf_op jit(solution)/shard_map/block/pallas_call | solution.py:354
  46.8 0.0 copy-start.1
  46.8 10.5 %regroup.1.got = bf16[8,64,256]{2,1,0:T(8,128)(2,1)} custom-call(bf16[8,64,256]{2,1,0:T(8,128)(2,1)} %block.1.send), custom_call_target="tpu_custom_call" | custom-call | tf_op jit(solution)/shard_map/regroup/pallas_call | solution.py:366
  57.3 0.0 copy-done.1
  57.4 0.7 reshape.14.table
  58.1 10.0 %grid.1.send = bf16[8,4,4,8,128]{4,3,2,1,0:T(8,128)(2,1)} custom-call(bf16[8,64,256]{2,1,0:T(8,128)(2,1)} %regroup.1.got, f32[1,256]{1,0:T(1,128)} %bitcast.12, bf16[256,768]{1,0:T(8,128)(2,1)} %qkv.3, bf16[256,256]{1,0:T(8,128)(2,1)} %merge.3, f32[8,256]{1,0:T(8,128)} %reshape.14.table, f32[1,256]{1,0:T(1,128)} %bitcast.13, bf16[256,1024]{1,0:T(8,128)(2,1)} %up.1, ...), custom_call_target="tpu_custom_call" | custom-call | tf_op jit(solution)/shard_map/grid/pallas_call | solution.py:354
  68.1 17.3 %home.1.got = bf16[8,4,4,8,128]{4,3,2,1,0:T(8,128)(2,1)} custom-call(bf16[8,4,4,8,128]{4,3,2,1,0:T(8,128)(2,1)} %grid.1.send), custom_call_target="tpu_custom_call" | custom-call | tf_op jit(solution)/shard_map/home/pallas_call | solution.py:366
  85.4 2.1 %finish.1 = bf16[8,64,256]{2,1,0:T(8,128)(2,1)} custom-call(bf16[8,4,4,8,128]{4,3,2,1,0:T(8,128)(2,1)} %home.1.got), custom_call_target="tpu_custom_call" | custom-call | tf_op jit(solution)/shard_map/finish/pallas_call | solution.py:354
  87.5 1.8 %copy.23 = bf16[64,8,256]{2,1,0:T(8,128)(2,1)} copy(bf16[64,8,256]{2,0,1:T(8,128)(2,1)} %bitcast.11) | data formatting | bytes 524288 | tf_op jit(solution)/shard_map/transpose | solution.py:446
  (4 shorter events, 0.0 us)
Async XLA Ops:
  4.6 26.5 %copy-start = (f32[8,15,15]{2,0,1:T(8,128)S(1)}, f32[8,15,15]{2,0,1:T(8,128)}, u32[]{:S(2)}) copy-start(f32[8,15,15]{2,0,1:T(8,128)} %param.27) | copy-start | bytes 21604
  31.1 0.7 copy-start.2
  46.8 10.5 %copy-start.1 = (f32[8,15,15]{2,0,1:T(8,128)S(1)}, f32[8,15,15]{2,0,1:T(8,128)}, u32[]{:S(2)}) copy-start(f32[8,15,15]{2,0,1:T(8,128)} %param.31) | copy-start | bytes 21604
where the time goes:
time: 89.8 us; the launch traced here: 89.3 us
  Pallas kernels  83 us (92%)
  local copies, waits for them, and re-layouts  5.6 us (6%)
    pallas_call x3, Pallas kernels, exchange(): pl.pallas_call(body, out_shape=jax.ShapeDtypeStruct(shape, BF16), in_spec...  54.3 us
    pallas_call x4, Pallas kernels, local(): pl.pallas_call(body, out_shape=jax.ShapeDtypeStruct(shape, dtype), in_spe...  28.7 us
    transpose x1, local copies, waits for them, and re-layouts, shards(): return jnp.transpose(out, (1, 0, 2))  1.8 us

commit v1 on v0

v1 whole, which is shorter than its diff:
```python
import functools
import math

import jax
import jax.numpy as jnp
import numpy as np
from jax import lax
from jax.experimental import pallas as pl
from jax.experimental.pallas import tpu as pltpu
from jax.sharding import PartitionSpec as P

WIN = 8
HALF = 64
EPS = 1e-05
F32 = jnp.float32
BF16 = jnp.bfloat16
MESH = pl.DeviceIdType.MESH
VM = pl.BlockSpec(memory_space=pltpu.VMEM)
LIMIT = 56 * 1024 * 1024


def dot(a, b, dims=((1,), (0,))):
    return lax.dot_general(a, b, (dims, ((), ())), preferred_element_type=F32)


def norm(values, gain):
    middle = jnp.mean(values, axis=-1, keepdims=True)
    off = values - middle
    spread = jnp.mean(off * off, axis=-1, keepdims=True)
    return (off * lax.rsqrt(spread + EPS) * gain).astype(BF16)


def gelu(v):
    return 0.5 * v * (1.0 + lax.erf(v * np.float32(math.sqrt(0.5))))


def rounded(v):
    return v.astype(BF16).astype(F32)


def swapped(v):
    return pltpu.roll(v, HALF, 1)


def pick_rows(lanes):
    width = 4 * lanes * WIN
    first = np.zeros((lanes * 40, width), np.float32)
    second = np.zeros((lanes * 40, width), np.float32)
    mask = np.zeros((lanes * 40, 128), np.float32)
    for j in range(lanes):
        for q in range(40):
            if q < 32:
                col = (q // 8 * lanes + j) * 8 + q % 8
            else:
                col = ((q - 32) % 4 * lanes + j) * 8 + (-1 if q < 36 else 8)
            row = j * 40 + q
            if col < 0:
                second[row, width - 1] = 1
                mask[row, HALF:] = 1
            elif col >= width:
                second[row, 0] = 1
                mask[row, :HALF] = 1
            else:
                first[row, col] = 1
    return first, second, mask


def prep_body(px, first, second, mask, send):
    half = px.shape[2] // 2
    lanes = send.shape[0]
    for y in range(WIN):
        low, high = px[y, :, :half], px[y, :, half:]
        main = dot(first[...], jnp.concatenate([low, high], 0), ((1,), (1,)))
        rim = dot(second[...], jnp.concatenate([high, low], 0), ((1,), (1,)))
        rows = (main + rim * mask[...]).astype(BF16)
        for j in range(lanes):
            send[j, y] = rows[j * 40 : (j + 1) * 40]


def bias_fill(table, flat, bias):
    flat[...] = jnp.zeros_like(flat)
    for i in range(2 * WIN - 1):
        flat[:, i * 16 : i * 16 + 15] = table[:, i, :]
    t = flat[...]
    shifted = [t if z == 0 else pltpu.roll(t, 256 - z * 16, 1) for z in range(WIN)]
    rows = jnp.concatenate([s[:, :128] for s in shifted], 0)
    r = lax.broadcasted_iota(jnp.int32, (128, 128), 0)
    c = lax.broadcasted_iota(jnp.int32, (128, 128), 1)
    m, j = r >> 4, r & 15
    y, x = (c >> 3) & 7, c & 7
    for v in range(WIN):
        onehot = jnp.where((m == 7 - y) & (j == v - x + 7), 1.0, 0.0).astype(F32)
        got = lax.dot_general(
            rows, onehot, (((1,), (0,)), ((), ())),
            precision=lax.Precision.HIGHEST, preferred_element_type=F32,
        )
        bias[:, v] = got.reshape(WIN, WIN, 128)


def attend_pair(x, gain, qkv, merge, bias):
    channels = x.shape[1]
    depth = channels // WIN
    proj = dot(norm(x, gain), qkv)
    q = proj[:, :channels].astype(BF16)
    head = lax.broadcasted_iota(jnp.int32, (WIN, channels), 0)
    place = lax.broadcasted_iota(jnp.int32, (WIN, channels), 1)
    own = jnp.where((place >= head * depth) & (place < head * depth + depth), 1.0, 0.0)

    def spread(rows):
        wide = rounded(rows)[:, None, :] * own[None]
        return wide.reshape(64 * WIN, channels).astype(BF16)

    keys = [spread(proj[w * 64 : w * 64 + 64, channels : 2 * channels]) for w in (0, 1)]
    vals = [spread(proj[w * 64 : w * 64 + 64, 2 * channels :]) for w in (0, 1)]
    raw = [dot(k, q, ((1,), (1,))) for k in keys]
    lane = lax.broadcasted_iota(jnp.int32, raw[0].shape, 1)
    scores = jnp.where(lane < 64, raw[0], raw[1]) * np.float32(1.0 / math.sqrt(depth))
    scores = scores.reshape(64, WIN, 128) + bias[...].reshape(64, WIN, 128)
    raised = jnp.exp(scores - jnp.max(scores, axis=0, keepdims=True))
    weights = raised * (1.0 / jnp.sum(raised, axis=0, keepdims=True))
    weights = jnp.transpose(weights.reshape(512, 128)).astype(BF16)
    heads = jnp.concatenate([dot(weights[w * 64 : w * 64 + 64], vals[w]) for w in (0, 1)], 0)
    return rounded(x + dot(heads.astype(BF16), merge))


def conv_phase(at_top, at_end, got, gain, expand, taps, shrink, tokens, normed, acc):
    lanes = got.shape[0]
    lane = lax.broadcasted_iota(jnp.int32, (400, 128), 1)
    row = lax.broadcasted_iota(jnp.int32, (400, 128), 0)
    lowest = jnp.where(at_top, 40, 0)
    highest = jnp.where(at_end, 360, 400)
    keep = (row >= lowest) & (row < highest)
    for i in range(0, lanes, 2):
        a = jnp.where(keep, got[i].astype(F32).reshape(400, 128), 0.0)
        b = jnp.where(keep, got[i + 1].astype(F32).reshape(400, 128), 0.0)
        cols = slice(i * HALF, i * HALF + 128)
        tokens[:400, cols] = jnp.where(lane < HALF, a, swapped(b))
        tokens[400:, cols] = jnp.where(lane < HALF, swapped(a), b)
    for half in (0, 1):
        normed[half * 400 : half * 400 + 400] = norm(
            tokens[half * 400 : half * 400 + 400], gain[...]
        )
    for half in (0, 1):
        for y in range(WIN):
            base = half * 400 + (y + 1) * 40
            acc[half * 256 + y * 32 : half * 256 + y * 32 + 32] = tokens[base : base + 32]

    width = 128
    inner = lax.broadcasted_iota(jnp.int32, (WIN, WIN, width), 1)

    def chunk(n, _):
        at = pl.ds(pl.multiple_of(n * width, width), width)
        kernel = taps[:, :, at].astype(F32)
        for half in (0, 1):
            wide = rounded(gelu(dot(normed[half * 400 : half * 400 + 400], expand[:, at])))
            wide = wide.reshape(10, 5, 8, width)

            def column(v, tile):
                total = None
                for u in range(3):
                    term = wide[u : u + WIN, tile] * kernel[u, v][None, None, :]
                    total = term if total is None else total + term
                return total

            left_rim, right_rim = column(0, 4), column(2, 4)
            parts = []
            for b in range(4):
                left = jnp.where(
                    inner == 0, left_rim[:, b : b + 1], pltpu.roll(column(0, b), 1, 1)
                )
                right = jnp.where(
                    inner == 7, right_rim[:, 4 + b : 5 + b], pltpu.roll(column(2, b), 7, 1)
                )
                parts.append(column(1, b) + left + right)
            summed = jnp.stack(parts, axis=1).reshape(256, width)
            narrow = dot(gelu(summed).astype(BF16), shrink[at, :])
            acc[half * 256 : half * 256 + 256] += narrow
        return _

    lax.fori_loop(0, expand.shape[1] // width, chunk, 0)


def window_pair(n, gain, qkv, merge, bias, acc, done, send):
    channels = acc.shape[1]
    groups = []
    for w in (0, 1):
        b = n * 2 + w
        base = (b >> 2) * 256 + (b & 3) * 8
        groups += [acc[pl.ds(pl.multiple_of(base + y * 32, 8), 8)] for y in range(WIN)]
    x = rounded(jnp.concatenate(groups, 0))
    out = attend_pair(x, gain[...], qkv[...], merge[...], bias)
    for c in range(channels // 128):
        cols = slice(c * 128, c * 128 + 128)
        done[c] = out[:, cols]
        for x in range(WIN):
            send[x, n, :, cols] = done[c, pl.ds(x, 16, stride=8)].astype(BF16)


def group_pair(n, gain, qkv, merge, bias, mlp_gain, up, down, tokens, send):
    parts = tokens.shape[0]
    lane = lax.broadcasted_iota(jnp.int32, (64, 128), 1)
    halves = [
        jnp.concatenate([tokens[c, pl.ds(n + w * 4, 64, stride=8)] for c in range(parts)], 1)
        for w in (0, 1)
    ]
    x = attend_pair(jnp.concatenate(halves, 0), gain[...], qkv[...], merge[...], bias)
    hidden = gelu(dot(norm(x, mlp_gain[...]), up[...])).astype(BF16)
    out = rounded(x + dot(hidden, down[...]))
    for c in range(parts):
        low, high = out[:64, c * 128 : c * 128 + 128], out[64:, c * 128 : c * 128 + 128]
        even = jnp.where(lane < HALF, low, swapped(high))
        odd = jnp.where(lane < HALF, swapped(low), high)
        send[:, 2 * c, n] = even.reshape(WIN, WIN, 128).astype(BF16)
        send[:, 2 * c + 1, n] = odd.reshape(WIN, WIN, 128).astype(BF16)


def finish_chunk(n, got, rows, out):
    lanes = got.shape[1]
    for x in range(WIN):
        for j in range(lanes):
            rows[pl.ds(j * 8 + x, 8, stride=8 * lanes)] = got[x, j, n].astype(F32)
    flat = jnp.transpose(rows[...]).astype(BF16)
    out[n] = flat[:HALF]
    out[n + 4] = flat[HALF:]


def whole_body(
    bands, lanes,
    px, first, second, mask, conv_gain, expand, taps, shrink,
    block_gain, block_qkv, block_merge, block_table,
    grid_gain, grid_qkv, grid_merge, grid_table, mlp_gain, up, down,
    out,
    send0, got0, tokens, normed, acc, flat, block_bias, grid_bias, done,
    send1, got1, columns, send2, got2, rows,
    ss0, rs0, os0, ss1, rs1, os1, ss2, rs2, os2,
):
    band, lane = lax.axis_index("rows"), lax.axis_index("ch")
    step = bands // WIN
    slot, rest = band // step, lax.rem(band, step)
    below, above = lax.rem(band + 1, bands), lax.rem(band + bands - 1, bands)
    lane_at = [lax.rem(lane + d, lanes) for d in range(lanes)]
    slot_at = [lax.rem(slot + d, WIN) for d in range(WIN)]
    band_at = [s * step + rest for s in slot_at]
    pairs = [(d, e) for d in range(WIN) for e in range(lanes) if d or e]
    barrier = pltpu.get_barrier_semaphore()
    partners = [(row, j) for row in (below, above) for j in lane_at]
    partners += [(band_at[d], lane_at[e]) for d, e in pairs]
    for partner in partners:
        pl.semaphore_signal(barrier, inc=1, device_id=partner, device_id_type=MESH)
    prep_body(px, first, second, mask, send0)
    pl.semaphore_wait(barrier, len(partners))

    def spread(kind, d, mine):
        row = (band, below, above)[kind]
        if kind == 0:
            src, dst = send0.at[lane_at[d]], got0.at[mine, pl.ds(1, WIN)]
        else:
            src = send0.at[lane_at[d], WIN - 1 if kind == 1 else 0]
            dst = got0.at[mine, 0 if kind == 1 else WIN + 1]
        return pltpu.make_async_remote_copy(
            src_ref=src, dst_ref=dst, send_sem=ss0.at[kind, d], recv_sem=rs0.at[kind, mine],
            device_id=(row, lane_at[d]), device_id_type=MESH,
        )

    spreads = [(k, d) for k in range(3) for d in range(lanes) if k or d]
    for k, d in spreads:
        spread(k, d, lane).start()
    own = pltpu.make_async_copy(send0.at[lane], got0.at[lane, pl.ds(1, WIN)], os0)
    own.start()
    bias_fill(block_table, flat, block_bias)
    bias_fill(grid_table, flat, grid_bias)
    own.wait()
    for k, d in spreads:
        spread(k, d, lane_at[d]).wait_recv()
    conv_phase(
        band == 0, band == bands - 1, got0, conv_gain, expand, taps, shrink, tokens, normed, acc
    )

    def regroup(n, d, mine):
        return pltpu.make_async_remote_copy(
            src_ref=send1.at[slot_at[d], n], dst_ref=got1.at[mine, n],
            send_sem=ss1.at[n, d], recv_sem=rs1.at[n, mine],
            device_id=(band_at[d], lane), device_id_type=MESH,
        )

    def regroup_own(n):
        return pltpu.make_async_copy(send1.at[slot, n], got1.at[slot, n], os1.at[n])

    def windows(n, _):
        window_pair(n, block_gain, block_qkv, block_merge, block_bias, acc, done, send1)
        for d in range(1, WIN):
            regroup(n, d, slot).start()
        regroup_own(n).start()
        return _

    lax.fori_loop(0, 4, windows, 0)

    def arrive(n, _):
        regroup_own(n).wait()
        for d in range(1, WIN):
            regroup(n, d, slot_at[d]).wait_recv()
        for a in range(WIN):
            part = got1[a, n].astype(F32)
            for c in range(columns.shape[0]):
                columns[c, pl.ds(pl.multiple_of(a * 64 + n * 16, 16), 16)] = part[
                    :, c * 128 : c * 128 + 128
                ]
        return _

    lax.fori_loop(0, 4, arrive, 0)

    def home(n, d, e, from_slot, from_lane):
        return pltpu.make_async_remote_copy(
            src_ref=send2.at[slot_at[d], lane_at[e], n], dst_ref=got2.at[from_slot, from_lane, n],
            send_sem=ss2.at[n, d, e], recv_sem=rs2.at[n, from_slot, from_lane],
            device_id=(band_at[d], lane_at[e]), device_id_type=MESH,
        )

    def home_own(n):
        return pltpu.make_async_copy(
            send2.at[slot, lane, n], got2.at[slot, lane, n], os2.at[n]
        )

    def groups(n, _):
        group_pair(
            n, grid_gain, grid_qkv, grid_merge, grid_bias, mlp_gain, up, down, columns, send2
        )
        for d, e in pairs:
            home(n, d, e, slot, lane).start()
        home_own(n).start()
        return _

    lax.fori_loop(0, 4, groups, 0)

    def finish(n, _):
        home_own(n).wait()
        for d, e in pairs:
            home(n, d, e, slot_at[d], lane_at[e]).wait_recv()
        finish_chunk(n, got2, rows, out)
        return _

    lax.fori_loop(0, 4, finish, 0)
    for k, d in spreads:
        spread(k, d, lane).wait_send()

    def sent(n, _):
        for d in range(1, WIN):
            regroup(n, d, slot).wait_send()
        for d, e in pairs:
            home(n, d, e, slot, lane).wait_send()
        return _

    lax.fori_loop(0, 4, sent, 0)


def shards(
    pixels, conv_gain, expand_weight, depth_kernel, shrink_weight,
    block_gain, block_qkv, block_merge, block_bias,
    grid_gain, grid_qkv, grid_merge, grid_bias, mlp_gain, mlp_up, mlp_down,
):
    lanes, bands = lax.axis_size("ch"), lax.axis_size("rows")
    channels = expand_weight.shape[0]
    columns = pixels.shape[2]
    first, second, mask = pick_rows(lanes)
    operands = [
        jnp.transpose(pixels, (1, 0, 2)),
        jnp.asarray(first, BF16), jnp.asarray(second, BF16), jnp.asarray(mask, F32),
        conv_gain[None], expand_weight, depth_kernel, shrink_weight,
        block_gain[None], block_qkv, block_merge, block_bias,
        grid_gain[None], grid_qkv, grid_merge, grid_bias,
        mlp_gain[None], mlp_up, mlp_down,
    ]
    dma = pltpu.SemaphoreType.DMA
    out = pl.pallas_call(
        functools.partial(whole_body, bands, lanes),
        out_shape=jax.ShapeDtypeStruct((WIN, HALF, columns), BF16),
        in_specs=[VM] * len(operands),
        out_specs=VM,
        scratch_shapes=[
            pltpu.VMEM((lanes, WIN, 40, 128), BF16),
            pltpu.VMEM((lanes, WIN + 2, 40, 128), BF16),
            pltpu.VMEM((800, channels), F32),
            pltpu.VMEM((800, channels), BF16),
            pltpu.VMEM((512, channels), F32),
            pltpu.VMEM((WIN, 256), F32),
            pltpu.VMEM((WIN, WIN, WIN, 128), F32),
            pltpu.VMEM((WIN, WIN, WIN, 128), F32),
            pltpu.VMEM((channels // 128, 128, 128), F32),
            pltpu.VMEM((WIN, 4, 16, channels), BF16),
            pltpu.VMEM((WIN, 4, 16, channels), BF16),
            pltpu.VMEM((channels // 128, 512, 128), F32),
            pltpu.VMEM((WIN, lanes, 4, WIN, 128), BF16),
            pltpu.VMEM((WIN, lanes, 4, WIN, 128), BF16),
            pltpu.VMEM((columns, 128), F32),
            dma((3, lanes)), dma((3, lanes)), dma,
            dma((4, WIN)), dma((4, WIN)), dma((4,)),
            dma((4, WIN, lanes)), dma((4, WIN, lanes)), dma((4,)),
        ],
        compiler_params=pltpu.CompilerParams(
            collective_id=1, has_side_effects=True, vmem_limit_bytes=LIMIT
        ),
        name="maxvit",
    )(*operands)
    return jnp.transpose(out, (1, 0, 2))


def solution(mesh):
    in_specs = (P("ch", "rows", None),) + (P(),) * 15
    return jax.shard_map(
        shards, mesh=mesh, in_specs=in_specs, out_specs=P("ch", "rows", None), check_vma=False
    )
```

time: 89.8 us -> 70 us (0.78)
  the two profiles are of different devices: /device:TPU:1 before, /device:TPU:2 now
where the time goes in v1:
time: 70 us; the launch traced here: 69.8 us
  Pallas kernels  64.2 us (92%)
  local copies, waits for them, and re-layouts  5.6 us (8%)
    pallas_call x1, Pallas kernels, shards(): pl.pallas_call(functools.partial(whole_body, bands, lanes), out_shape=jax...  64.2 us
    unnamed x5, local copies, waits for them, and re-layouts  3.8 us
    transpose x1, local copies, waits for them, and re-layouts, shards(): return jnp.transpose(out, (1, 0, 2))  1.8 us

profile of v1, /device:TPU:2, one launch (start us, length us, event | category | flops | bytes accessed | tf_op | source)
XLA Modules:
  0.0 69.8 jit_solution(509895805725618088)
XLA Ops:
  0.0 0.0 copy-start
  0.0 1.5 %copy.21.block_table = f32[8,15,15]{2,1,0:T(8,128)} copy(f32[8,15,15]{2,0,1:T(8,128)} %param.27) | data formatting | bytes 14400 | tf_op args[8]
  1.5 0.0 copy-done
  1.5 0.6 copy.22.grid_table
  2.1 1.7 %copy.25 = bf16[64,8,256]{2,0,1:T(8,128)(2,1)} copy(bf16[64,8,256]{2,1,0:T(8,128)(2,1)} %param.19) | data formatting | bytes 524288 | tf_op args[0]
  3.8 64.2 %maxvit.1 = bf16[8,64,256]{2,1,0:T(8,128)(2,1)} custom-call(bf16[8,64,256]{2,1,0:T(8,128)(2,1)} %bitcast.9, bf16[160,128]{1,0:T(8,128)(2,1)} %constant.6.clone.first, bf16[160,128]{1,0:T(8,128)(2,1)} %constant.7.clone.second, f32[160,128]{1,0:T(8,128)} %constant.8.clone.mask, f32[1,256]{1,0:T(1,128)} %bitcast.10, bf16[256,1024]{1,0:T(8,128)(2,1)} %expand.1, ...), custom_call_target="tpu_custom_call" | custom-call | tf_op jit(solution)/shard_map/maxvit/pallas_call | solution.py:374
  68.0 1.8 %copy.23 = bf16[64,8,256]{2,1,0:T(8,128)(2,1)} copy(bf16[64,8,256]{2,0,1:T(8,128)(2,1)} %bitcast.8) | data formatting | bytes 524288 | tf_op jit(solution)/shard_map/transpose | solution.py:404
Async XLA Ops:
  0.0 1.5 %copy-start = (f32[8,15,15]{2,0,1:T(8,128)S(1)}, f32[8,15,15]{2,0,1:T(8,128)}, u32[]{:S(2)}) copy-start(f32[8,15,15]{2,0,1:T(8,128)} %param.31) | copy-start | bytes 21604

commit v2 on v1

--- a/solution.py
+++ b/solution.py
@@ -30,8 +30,8 @@
     return (off * lax.rsqrt(spread + EPS) * gain).astype(BF16)
 
 
-def gelu(v):
-    return 0.5 * v * (1.0 + lax.erf(v * np.float32(math.sqrt(0.5))))
+def twice_gelu(v):
+    return v * (1.0 + lax.erf(v * np.float32(math.sqrt(0.5))))
 
 
 def rounded(v):
@@ -65,11 +65,16 @@
     return first, second, mask
 
 
-def prep_body(px, first, second, mask, send):
+def prep_body(px, first, second, mask, plane, send):
     half = px.shape[2] // 2
     lanes = send.shape[0]
+    for c in range(plane.shape[0]):
+        part = px[:, :, c * 128 : c * 128 + 128].astype(F32)
+        plane[c] = part.reshape(HALF * WIN, 128)
     for y in range(WIN):
-        low, high = px[y, :, :half], px[y, :, half:]
+        line = [plane[c, pl.ds(y, HALF, stride=WIN)] for c in range(plane.shape[0])]
+        line = jnp.concatenate(line, 1).astype(BF16)
+        low, high = line[:, :half], line[:, half:]
         main = dot(first[...], jnp.concatenate([low, high], 0), ((1,), (1,)))
         rim = dot(second[...], jnp.concatenate([high, low], 0), ((1,), (1,)))
         rows = (main + rim * mask[...]).astype(BF16)
@@ -80,7 +85,7 @@
 def bias_fill(table, flat, bias):
     flat[...] = jnp.zeros_like(flat)
     for i in range(2 * WIN - 1):
-        flat[:, i * 16 : i * 16 + 15] = table[:, i, :]
+        flat[:, i * 16 : i * 16 + 15] = table[i]
     t = flat[...]
     shifted = [t if z == 0 else pltpu.roll(t, 256 - z * 16, 1) for z in range(WIN)]
     rows = jnp.concatenate([s[:, :128] for s in shifted], 0)
@@ -145,14 +150,14 @@
             base = half * 400 + (y + 1) * 40
             acc[half * 256 + y * 32 : half * 256 + y * 32 + 32] = tokens[base : base + 32]
 
-    width = 128
+    width = min(512, expand.shape[1])
     inner = lax.broadcasted_iota(jnp.int32, (WIN, WIN, width), 1)
 
     def chunk(n, _):
         at = pl.ds(pl.multiple_of(n * width, width), width)
-        kernel = taps[:, :, at].astype(F32)
+        kernel = taps[:, :, at].astype(F32) * 0.5
         for half in (0, 1):
-            wide = rounded(gelu(dot(normed[half * 400 : half * 400 + 400], expand[:, at])))
+            wide = twice_gelu(dot(normed[half * 400 : half * 400 + 400], expand[:, at]))
             wide = wide.reshape(10, 5, 8, width)
 
             def column(v, tile):
@@ -173,8 +178,8 @@
                 )
                 parts.append(column(1, b) + left + right)
             summed = jnp.stack(parts, axis=1).reshape(256, width)
-            narrow = dot(gelu(summed).astype(BF16), shrink[at, :])
-            acc[half * 256 : half * 256 + 256] += narrow
+            narrow = dot(twice_gelu(summed).astype(BF16), shrink[at, :])
+            acc[half * 256 : half * 256 + 256] += 0.5 * narrow
         return _
 
     lax.fori_loop(0, expand.shape[1] // width, chunk, 0)
@@ -204,8 +209,8 @@
         for w in (0, 1)
     ]
     x = attend_pair(jnp.concatenate(halves, 0), gain[...], qkv[...], merge[...], bias)
-    hidden = gelu(dot(norm(x, mlp_gain[...]), up[...])).astype(BF16)
-    out = rounded(x + dot(hidden, down[...]))
+    hidden = twice_gelu(dot(norm(x, mlp_gain[...]), up[...])).astype(BF16)
+    out = rounded(x + 0.5 * dot(hidden, down[...]))
     for c in range(parts):
         low, high = out[:64, c * 128 : c * 128 + 128], out[64:, c * 128 : c * 128 + 128]
         even = jnp.where(lane < HALF, low, swapped(high))
@@ -226,11 +231,13 @@
 
 def whole_body(
     bands, lanes,
-    px, first, second, mask, conv_gain, expand, taps, shrink,
-    block_gain, block_qkv, block_merge, block_table,
-    grid_gain, grid_qkv, grid_merge, grid_table, mlp_gain, up, down,
+    px, first, second, mask, conv_gain, taps, block_gain, block_table,
+    grid_gain, grid_table, mlp_gain,
+    expand_far, shrink_far, block_qkv_far, block_merge_far,
+    grid_qkv_far, grid_merge_far, up_far, down_far,
     out,
-    send0, got0, tokens, normed, acc, flat, block_bias, grid_bias, done,
+    expand, shrink, block_qkv, block_merge, grid_qkv, grid_merge, up, down, loaded,
+    plane, send0, got0, tokens, normed, acc, flat, block_bias, grid_bias, done,
     send1, got1, columns, send2, got2, rows,
     ss0, rs0, os0, ss1, rs1, os1, ss2, rs2, os2,
 ):
@@ -247,7 +254,17 @@
     partners += [(band_at[d], lane_at[e]) for d, e in pairs]
     for partner in partners:
         pl.semaphore_signal(barrier, inc=1, device_id=partner, device_id_type=MESH)
-    prep_body(px, first, second, mask, send0)
+    far = (
+        expand_far, shrink_far, block_qkv_far, block_merge_far,
+        grid_qkv_far, grid_merge_far, up_far, down_far,
+    )
+    near = (expand, shrink, block_qkv, block_merge, grid_qkv, grid_merge, up, down)
+    loads = [
+        pltpu.make_async_copy(f, m, loaded.at[i]) for i, (f, m) in enumerate(zip(far, near))
+    ]
+    for load in loads:
+        load.start()
+    prep_body(px, first, second, mask, plane, send0)
     pl.semaphore_wait(barrier, len(partners))
 
     def spread(kind, d, mine):
@@ -270,6 +287,8 @@
     bias_fill(block_table, flat, block_bias)
     bias_fill(grid_table, flat, grid_bias)
     own.wait()
+    for load in loads:
+        load.wait()
     for k, d in spreads:
         spread(k, d, lane_at[d]).wait_recv()
     conv_phase(
@@ -363,20 +382,26 @@
     columns = pixels.shape[2]
     first, second, mask = pick_rows(lanes)
     operands = [
-        jnp.transpose(pixels, (1, 0, 2)),
+        pixels,
         jnp.asarray(first, BF16), jnp.asarray(second, BF16), jnp.asarray(mask, F32),
-        conv_gain[None], expand_weight, depth_kernel, shrink_weight,
-        block_gain[None], block_qkv, block_merge, block_bias,
-        grid_gain[None], grid_qkv, grid_merge, grid_bias,
-        mlp_gain[None], mlp_up, mlp_down,
+        conv_gain[None], depth_kernel,
+        block_gain[None], jnp.transpose(block_bias, (1, 0, 2)),
+        grid_gain[None], jnp.transpose(grid_bias, (1, 0, 2)), mlp_gain[None],
+    ]
+    weights = [
+        expand_weight, shrink_weight, block_qkv, block_merge,
+        grid_qkv, grid_merge, mlp_up, mlp_down,
     ]
     dma = pltpu.SemaphoreType.DMA
     out = pl.pallas_call(
         functools.partial(whole_body, bands, lanes),
         out_shape=jax.ShapeDtypeStruct((WIN, HALF, columns), BF16),
-        in_specs=[VM] * len(operands),
+        in_specs=[VM] * len(operands) + [pl.BlockSpec(memory_space=pl.ANY)] * len(weights),
         out_specs=VM,
-        scratch_shapes=[
+        scratch_shapes=[pltpu.VMEM(w.shape, w.dtype) for w in weights]
+        + [
+            dma((len(weights),)),
+            pltpu.VMEM((columns // 128, HALF * WIN, 128), F32),
             pltpu.VMEM((lanes, WIN, 40, 128), BF16),
             pltpu.VMEM((lanes, WIN + 2, 40, 128), BF16),
             pltpu.VMEM((800, channels), F32),
@@ -400,7 +425,7 @@
             collective_id=1, has_side_effects=True, vmem_limit_bytes=LIMIT
         ),
         name="maxvit",
-    )(*operands)
+    )(*operands, *weights)
     return jnp.transpose(out, (1, 0, 2))
 
 

time: 70 us -> 62.1 us (0.89)
  Pallas kernels: 64.2 us -> 60.1 us
  local copies, waits for them, and re-layouts: 5.6 us -> 1.8 us
    pallas_call x1, Pallas kernels: 64.2 us -> 60.1 us  [shards(): pl.pallas_call(functools.partial(whole_body, bands, lanes), out_shape=jax...]
    unnamed x5 -> x0, local copies, waits for them, and re-layouts: 3.8 us -> none
where the time goes in v2:
time: 62.1 us; the launch traced here: 61.9 us
  Pallas kernels  60.1 us (97%)
  local copies, waits for them, and re-layouts  1.8 us (3%)
    pallas_call x1, Pallas kernels, shards(): pl.pallas_call(functools.partial(whole_body, bands, lanes), out_shape=jax...  60.1 us
    transpose x1, local copies, waits for them, and re-layouts, shards(): return jnp.transpose(out, (1, 0, 2))  1.8 us

profile of v2, /device:TPU:2, one launch (start us, length us, event | category | flops | bytes accessed | tf_op | source)
XLA Modules:
  0.0 61.9 jit_solution(17451715432510240388)
XLA Ops:
  0.0 60.1 %maxvit.1 = bf16[8,64,256]{2,1,0:T(8,128)(2,1)} custom-call(bf16[64,8,256]{2,1,0:T(8,128)(2,1)} %px.1, bf16[160,128]{1,0:T(8,128)(2,1)} %constant.6.clone.first, bf16[160,128]{1,0:T(8,128)(2,1)} %constant.7.clone.second, f32[160,128]{1,0:T(8,128)} %constant.8.clone.mask, f32[1,256]{1,0:T(1,128)} %bitcast.10, bf16[3,3,1024]{2,1,0:T(4,128)(2,1)} %taps.1, ...), custom_call_target="tpu_custom_call" | custom-call | tf_op jit(solution)/shard_map/maxvit/pallas_call | solution.py:396
  60.1 1.8 %copy.20 = bf16[64,8,256]{2,1,0:T(8,128)(2,1)} copy(bf16[64,8,256]{2,0,1:T(8,128)(2,1)} %bitcast.7) | data formatting | bytes 524288 | tf_op jit(solution)/shard_map/transpose | solution.py:429

commit v3 on v2

--- a/solution.py
+++ b/solution.py
@@ -99,7 +99,8 @@
             rows, onehot, (((1,), (0,)), ((), ())),
             precision=lax.Precision.HIGHEST, preferred_element_type=F32,
         )
-        bias[:, v] = got.reshape(WIN, WIN, 128)
+        for z in range(WIN):
+            bias[pl.ds(z * 8 + v, WIN, stride=64)] = got[z * 8 : z * 8 + 8]
 
 
 def attend_pair(x, gain, qkv, merge, bias):
@@ -107,22 +108,24 @@
     depth = channels // WIN
     proj = dot(norm(x, gain), qkv)
     q = proj[:, :channels].astype(BF16)
-    head = lax.broadcasted_iota(jnp.int32, (WIN, channels), 0)
-    place = lax.broadcasted_iota(jnp.int32, (WIN, channels), 1)
-    own = jnp.where((place >= head * depth) & (place < head * depth + depth), 1.0, 0.0)
+    place = lax.broadcasted_iota(jnp.int32, (1, channels), 1)
+    own = [
+        jnp.where((place >= h * depth) & (place < h * depth + depth), 1.0, 0.0).astype(BF16)
+        for h in range(WIN)
+    ]
 
     def spread(rows):
-        wide = rounded(rows)[:, None, :] * own[None]
-        return wide.reshape(64 * WIN, channels).astype(BF16)
+        rows = rows.astype(BF16)
+        return jnp.concatenate([rows * o for o in own], 0)
 
     keys = [spread(proj[w * 64 : w * 64 + 64, channels : 2 * channels]) for w in (0, 1)]
     vals = [spread(proj[w * 64 : w * 64 + 64, 2 * channels :]) for w in (0, 1)]
     raw = [dot(k, q, ((1,), (1,))) for k in keys]
     lane = lax.broadcasted_iota(jnp.int32, raw[0].shape, 1)
     scores = jnp.where(lane < 64, raw[0], raw[1]) * np.float32(1.0 / math.sqrt(depth))
-    scores = scores.reshape(64, WIN, 128) + bias[...].reshape(64, WIN, 128)
-    raised = jnp.exp(scores - jnp.max(scores, axis=0, keepdims=True))
-    weights = raised * (1.0 / jnp.sum(raised, axis=0, keepdims=True))
+    scores = (scores + bias[...]).reshape(WIN, 64, 128)
+    raised = jnp.exp(scores - jnp.max(scores, axis=1, keepdims=True))
+    weights = raised * (1.0 / jnp.sum(raised, axis=1, keepdims=True))
     weights = jnp.transpose(weights.reshape(512, 128)).astype(BF16)
     heads = jnp.concatenate([dot(weights[w * 64 : w * 64 + 64], vals[w]) for w in (0, 1)], 0)
     return rounded(x + dot(heads.astype(BF16), merge))
@@ -219,14 +222,15 @@
         send[:, 2 * c + 1, n] = odd.reshape(WIN, WIN, 128).astype(BF16)
 
 
-def finish_chunk(n, got, rows, out):
+def finish_chunk(n, got, rows, plane):
     lanes = got.shape[1]
     for x in range(WIN):
         for j in range(lanes):
             rows[pl.ds(j * 8 + x, 8, stride=8 * lanes)] = got[x, j, n].astype(F32)
-    flat = jnp.transpose(rows[...]).astype(BF16)
-    out[n] = flat[:HALF]
-    out[n + 4] = flat[HALF:]
+    for c in range(plane.shape[0]):
+        flat = jnp.transpose(rows[c * 128 : c * 128 + 128])
+        plane[c, pl.ds(n, HALF, stride=WIN)] = flat[:HALF]
+        plane[c, pl.ds(n + 4, HALF, stride=WIN)] = flat[HALF:]
 
 
 def whole_body(
@@ -355,10 +359,12 @@
         home_own(n).wait()
         for d, e in pairs:
             home(n, d, e, slot_at[d], lane_at[e]).wait_recv()
-        finish_chunk(n, got2, rows, out)
+        finish_chunk(n, got2, rows, plane)
         return _
 
     lax.fori_loop(0, 4, finish, 0)
+    for c in range(plane.shape[0]):
+        out[:, :, c * 128 : c * 128 + 128] = plane[c].reshape(HALF, WIN, 128).astype(BF16)
     for k, d in spreads:
         spread(k, d, lane).wait_send()
 
@@ -393,9 +399,9 @@
         grid_qkv, grid_merge, mlp_up, mlp_down,
     ]
     dma = pltpu.SemaphoreType.DMA
-    out = pl.pallas_call(
+    return pl.pallas_call(
         functools.partial(whole_body, bands, lanes),
-        out_shape=jax.ShapeDtypeStruct((WIN, HALF, columns), BF16),
+        out_shape=jax.ShapeDtypeStruct((HALF, WIN, columns), BF16),
         in_specs=[VM] * len(operands) + [pl.BlockSpec(memory_space=pl.ANY)] * len(weights),
         out_specs=VM,
         scratch_shapes=[pltpu.VMEM(w.shape, w.dtype) for w in weights]
@@ -408,8 +414,8 @@
             pltpu.VMEM((800, channels), BF16),
             pltpu.VMEM((512, channels), F32),
             pltpu.VMEM((WIN, 256), F32),
-            pltpu.VMEM((WIN, WIN, WIN, 128), F32),
-            pltpu.VMEM((WIN, WIN, WIN, 128), F32),
+            pltpu.VMEM((512, 128), F32),
+            pltpu.VMEM((512, 128), F32),
             pltpu.VMEM((channels // 128, 128, 128), F32),
             pltpu.VMEM((WIN, 4, 16, channels), BF16),
             pltpu.VMEM((WIN, 4, 16, channels), BF16),
@@ -426,7 +432,6 @@
         ),
         name="maxvit",
     )(*operands, *weights)
-    return jnp.transpose(out, (1, 0, 2))
 
 
 def solution(mesh):

time: 62.1 us -> 61 us (0.982)
  Pallas kernels: 60.1 us -> 59.1 us
    transpose x1 -> x0, local copies, waits for them, and re-layouts: 1.8 us -> none  [shards(): return jnp.transpose(out, (1, 0, 2))]
    unnamed x0 -> x1, local copies, waits for them, and re-layouts: none -> 1.67 us
    pallas_call x1, Pallas kernels: 60.1 us -> 59.1 us  [shards(): pl.pallas_call(functools.partial(whole_body, bands, lanes), out_shape=jax...]
where the time goes in v3:
time: 61 us; the launch traced here: 60.8 us
  Pallas kernels  59.1 us (97%)
  local copies, waits for them, and re-layouts  1.67 us (3%)
    pallas_call x1, Pallas kernels, shards(): pl.pallas_call(functools.partial(whole_body, bands, lanes), out_shape=jax...  59.1 us
    unnamed x1, local copies, waits for them, and re-layouts  1.67 us

profile of v3, /device:TPU:2, one launch (start us, length us, event | category | flops | bytes accessed | tf_op | source)
XLA Modules:
  0.0 60.8 jit_solution(10620588519734373734)
XLA Ops:
  0.0 59.1 %maxvit.1 = bf16[64,8,256]{2,1,0:T(8,128)(2,1)} custom-call(bf16[64,8,256]{2,1,0:T(8,128)(2,1)} %px.1, bf16[160,128]{1,0:T(8,128)(2,1)} %constant.6.clone.first, bf16[160,128]{1,0:T(8,128)(2,1)} %constant.7.clone.second, f32[160,128]{1,0:T(8,128)} %constant.8.clone.mask, f32[1,256]{1,0:T(1,128)} %bitcast.8, bf16[3,3,1024]{2,1,0:T(4,128)(2,1)} %taps.1, ...), custom_call_target="tpu_custom_call" | custom-call | tf_op jit(solution)/shard_map/maxvit/pallas_call | solution.py:402
  59.1 1.7 %copy.21 = bf16[64,8,256]{2,1,0:T(8,128)(2,1)} copy(bf16[64,8,256]{2,1,0:T(8,128)(2,1)} %maxvit.1) | data formatting | bytes 524288

commit v4 on v3

--- a/solution.py
+++ b/solution.py
@@ -131,42 +131,45 @@
     return rounded(x + dot(heads.astype(BF16), merge))
 
 
-def conv_phase(at_top, at_end, got, gain, expand, taps, shrink, tokens, normed, acc):
+def conv_phase(part, at_edge, got, gain, expand, taps, shrink, tokens, normed, acc):
     lanes = got.shape[0]
-    lane = lax.broadcasted_iota(jnp.int32, (400, 128), 1)
-    row = lax.broadcasted_iota(jnp.int32, (400, 128), 0)
-    lowest = jnp.where(at_top, 40, 0)
-    highest = jnp.where(at_end, 360, 400)
-    keep = (row >= lowest) & (row < highest)
+    lane = lax.broadcasted_iota(jnp.int32, (240, 128), 1)
+    row = lax.broadcasted_iota(jnp.int32, (240, 128), 0)
+    if part == 0:
+        keep = row >= jnp.where(at_edge, 40, 0)
+    else:
+        keep = row < jnp.where(at_edge, 200, 240)
+    own_rows = slice(part * 4, part * 4 + 6)
     for i in range(0, lanes, 2):
-        a = jnp.where(keep, got[i].astype(F32).reshape(400, 128), 0.0)
-        b = jnp.where(keep, got[i + 1].astype(F32).reshape(400, 128), 0.0)
+        a = jnp.where(keep, got[i, own_rows].astype(F32).reshape(240, 128), 0.0)
+        b = jnp.where(keep, got[i + 1, own_rows].astype(F32).reshape(240, 128), 0.0)
         cols = slice(i * HALF, i * HALF + 128)
-        tokens[:400, cols] = jnp.where(lane < HALF, a, swapped(b))
-        tokens[400:, cols] = jnp.where(lane < HALF, swapped(a), b)
+        tokens[:240, cols] = jnp.where(lane < HALF, a, swapped(b))
+        tokens[240:, cols] = jnp.where(lane < HALF, swapped(a), b)
     for half in (0, 1):
-        normed[half * 400 : half * 400 + 400] = norm(
-            tokens[half * 400 : half * 400 + 400], gain[...]
+        normed[half * 240 : half * 240 + 240] = norm(
+            tokens[half * 240 : half * 240 + 240], gain[...]
         )
     for half in (0, 1):
-        for y in range(WIN):
-            base = half * 400 + (y + 1) * 40
-            acc[half * 256 + y * 32 : half * 256 + y * 32 + 32] = tokens[base : base + 32]
+        for y in range(4):
+            base = half * 240 + (y + 1) * 40
+            at = half * 256 + part * 128 + y * 32
+            acc[at : at + 32] = tokens[base : base + 32]
 
     width = min(512, expand.shape[1])
-    inner = lax.broadcasted_iota(jnp.int32, (WIN, WIN, width), 1)
+    inner = lax.broadcasted_iota(jnp.int32, (4, WIN, width), 1)
 
     def chunk(n, _):
         at = pl.ds(pl.multiple_of(n * width, width), width)
         kernel = taps[:, :, at].astype(F32) * 0.5
         for half in (0, 1):
-            wide = twice_gelu(dot(normed[half * 400 : half * 400 + 400], expand[:, at]))
-            wide = wide.reshape(10, 5, 8, width)
+            wide = twice_gelu(dot(normed[half * 240 : half * 240 + 240], expand[:, at]))
+            wide = wide.reshape(6, 5, 8, width)
 
             def column(v, tile):
                 total = None
                 for u in range(3):
-                    term = wide[u : u + WIN, tile] * kernel[u, v][None, None, :]
+                    term = wide[u : u + 4, tile] * kernel[u, v][None, None, :]
                     total = term if total is None else total + term
                 return total
 
@@ -180,9 +183,10 @@
                     inner == 7, right_rim[:, 4 + b : 5 + b], pltpu.roll(column(2, b), 7, 1)
                 )
                 parts.append(column(1, b) + left + right)
-            summed = jnp.stack(parts, axis=1).reshape(256, width)
+            summed = jnp.stack(parts, axis=1).reshape(128, width)
             narrow = dot(twice_gelu(summed).astype(BF16), shrink[at, :])
-            acc[half * 256 : half * 256 + 256] += 0.5 * narrow
+            base = half * 256 + part * 128
+            acc[base : base + 128] += 0.5 * narrow
         return _
 
     lax.fori_loop(0, expand.shape[1] // width, chunk, 0)
@@ -272,9 +276,11 @@
     pl.semaphore_wait(barrier, len(partners))
 
     def spread(kind, d, mine):
-        row = (band, below, above)[kind]
+        row = (band, below, above, band)[kind]
         if kind == 0:
-            src, dst = send0.at[lane_at[d]], got0.at[mine, pl.ds(1, WIN)]
+            src, dst = send0.at[lane_at[d], pl.ds(0, 5)], got0.at[mine, pl.ds(1, 5)]
+        elif kind == 3:
+            src, dst = send0.at[lane_at[d], pl.ds(5, 3)], got0.at[mine, pl.ds(6, 3)]
         else:
             src = send0.at[lane_at[d], WIN - 1 if kind == 1 else 0]
             dst = got0.at[mine, 0 if kind == 1 else WIN + 1]
@@ -283,7 +289,7 @@
             device_id=(row, lane_at[d]), device_id_type=MESH,
         )
 
-    spreads = [(k, d) for k in range(3) for d in range(lanes) if k or d]
+    spreads = [(k, d) for k in (0, 1, 3, 2) for d in range(lanes) if k % 3 or d]
     for k, d in spreads:
         spread(k, d, lane).start()
     own = pltpu.make_async_copy(send0.at[lane], got0.at[lane, pl.ds(1, WIN)], os0)
@@ -293,11 +299,12 @@
     own.wait()
     for load in loads:
         load.wait()
-    for k, d in spreads:
-        spread(k, d, lane_at[d]).wait_recv()
-    conv_phase(
-        band == 0, band == bands - 1, got0, conv_gain, expand, taps, shrink, tokens, normed, acc
-    )
+    for part in (0, 1):
+        for k, d in spreads:
+            if k // 2 == part:
+                spread(k, d, lane_at[d]).wait_recv()
+        at_edge = band == (0 if part == 0 else bands - 1)
+        conv_phase(part, at_edge, got0, conv_gain, expand, taps, shrink, tokens, normed, acc)
 
     def regroup(n, d, mine):
         return pltpu.make_async_remote_copy(
@@ -410,8 +417,8 @@
             pltpu.VMEM((columns // 128, HALF * WIN, 128), F32),
             pltpu.VMEM((lanes, WIN, 40, 128), BF16),
             pltpu.VMEM((lanes, WIN + 2, 40, 128), BF16),
-            pltpu.VMEM((800, channels), F32),
-            pltpu.VMEM((800, channels), BF16),
+            pltpu.VMEM((480, channels), F32),
+            pltpu.VMEM((480, channels), BF16),
             pltpu.VMEM((512, channels), F32),
             pltpu.VMEM((WIN, 256), F32),
             pltpu.VMEM((512, 128), F32),
@@ -423,7 +430,7 @@
             pltpu.VMEM((WIN, lanes, 4, WIN, 128), BF16),
             pltpu.VMEM((WIN, lanes, 4, WIN, 128), BF16),
             pltpu.VMEM((columns, 128), F32),
-            dma((3, lanes)), dma((3, lanes)), dma,
+            dma((4, lanes)), dma((4, lanes)), dma,
             dma((4, WIN)), dma((4, WIN)), dma((4,)),
             dma((4, WIN, lanes)), dma((4, WIN, lanes)), dma((4,)),
         ],

time: 61 us -> 58.9 us (0.966)
  Pallas kernels: 59.1 us -> 57 us
    pallas_call x1, Pallas kernels: 59.1 us -> 57 us  [shards(): pl.pallas_call(functools.partial(whole_body, bands, lanes), out_shape=jax...]
where the time goes in v4:
time: 58.9 us; the launch traced here: 58.7 us
  Pallas kernels  57 us (97%)
  local copies, waits for them, and re-layouts  1.67 us (3%)
    pallas_call x1, Pallas kernels, shards(): pl.pallas_call(functools.partial(whole_body, bands, lanes), out_shape=jax...  57 us
    unnamed x1, local copies, waits for them, and re-layouts  1.67 us

profile of v4, /device:TPU:2, one launch (start us, length us, event | category | flops | bytes accessed | tf_op | source)
XLA Modules:
  0.0 58.7 jit_solution(18265139049560485343)
XLA Ops:
  0.0 57.0 %maxvit.1 = bf16[64,8,256]{2,1,0:T(8,128)(2,1)} custom-call(bf16[64,8,256]{2,1,0:T(8,128)(2,1)} %px.1, bf16[160,128]{1,0:T(8,128)(2,1)} %constant.6.clone.first, bf16[160,128]{1,0:T(8,128)(2,1)} %constant.7.clone.second, f32[160,128]{1,0:T(8,128)} %constant.8.clone.mask, f32[1,256]{1,0:T(1,128)} %bitcast.8, bf16[3,3,1024]{2,1,0:T(4,128)(2,1)} %taps.1, ...), custom_call_target="tpu_custom_call" | custom-call | tf_op jit(solution)/shard_map/maxvit/pallas_call | solution.py:409
  57.0 1.7 %copy.21 = bf16[64,8,256]{2,1,0:T(8,128)(2,1)} copy(bf16[64,8,256]{2,1,0:T(8,128)(2,1)} %maxvit.1) | data formatting | bytes 524288
